TPU v7x, 512 devices: a whole 4x4x16 slice. The times are simulated.
512 devices in a mesh: dom: 8 (over z_lo), orb: 64 (over x, y, z_hi, core).
Axes of the slice: x: 4, y: 4, z: 16 (z_hi: 2, z_lo: 8; z = z_hi * 8 + z_lo), core: 2. Of those that a mesh axis runs over, the one named last changes fastest.
Arguments:
- orbitals: float32 [8, 320, 12, 16, 128], P('dom', 'orb'), may hold values from -6 to 6
- potential: float32 [8, 12, 16, 128], P('dom'), may hold values from -3 to 0
- projectors: float32 [16, 8, 512], replicated, may hold values from -0.25 to 0.25
- projector_energy: float32 [8], replicated, may hold values from 20 to 160
- atom_first: int32 [16], replicated, may hold values from 0 to 23
- atom_second: int32 [16], replicated, may hold values from 0 to 31
- atom_third: int32 [16], replicated, may hold values from 0 to 255
- rotation: bfloat16 [320, 320], P('orb'), may hold values from -0.3125 to 0.3125
Outputs:
- rotated: bfloat16 [8, 320, 12, 16, 128], P('dom', 'orb')
All inputs are finite; a program needn't handle non-finite values.
Results may differ from a plain program's by a relative error of at most 0.0049.
Values may be sent and summed in bfloat16 or wider, within the bound.
A program may use at most 64 MiB of HBM per device.

v0:
```python
import jax
import jax.numpy as jnp
import numpy as np
from jax import lax
from jax.sharding import PartitionSpec as P

SIDE = 8
SUP = 512


stencil_weights = (
    -5369.0 / 1800.0,
    12.0 / 7.0,
    -15.0 / 56.0,
    10.0 / 189.0,
    -1.0 / 112.0,
    2.0 / 1925.0,
    -1.0 / 16632.0,
)
inverse_spacing = 4.0
filter_center = 120.0
filter_width = 110.0
stencil_reach = 6


def partner_2(block, axis, bit):
    count = lax.axis_size(axis)
    route = []
    for low in range(count):
        high = low | 1 << bit
        if high != low and high < count:
            route += [(low, high), (high, low)]
    return lax.ppermute(block, axis, route)


def outgoing(values, direction, width):
    extent = values.shape[direction]
    if 2 * width < extent:
        return jnp.concatenate(
            (
                lax.slice_in_dim(values, 0, width, axis=direction),
                lax.slice_in_dim(values, extent - width, extent, axis=direction),
            ),
            axis=direction,
        )
    return values


def assemble(values, partner, direction, width):
    extent = values.shape[direction]
    if 2 * width < extent:
        lower_rim = lax.slice_in_dim(partner, width, 2 * width, axis=direction)
        upper_rim = lax.slice_in_dim(partner, 0, width, axis=direction)
        return jnp.concatenate((lower_rim, values, upper_rim), axis=direction)
    cyclic = jnp.concatenate((values, partner), axis=direction)
    chosen = np.arange(-width, extent + width) % (2 * extent)
    return jnp.take(cyclic, jnp.asarray(chosen, dtype=jnp.int32), axis=direction)


def face_padded(values, direction, bit_number):
    sent = outgoing(values, direction, stencil_reach)
    partner = partner_2(sent.astype(jnp.bfloat16), "dom", bit_number).astype(sent.dtype)
    return assemble(values, partner, direction, stencil_reach)


def stencil_sum(center, along):
    lead = center.ndim - 3
    summed = 3.0 * stencil_weights[0] * center
    for index in range(3):
        direction = lead + index
        extent = center.shape[direction]
        padded = along[index]
        for offset in range(1, 7):
            upward = lax.slice_in_dim(
                padded, stencil_reach + offset, stencil_reach + offset + extent, axis=direction
            )
            downward = lax.slice_in_dim(
                padded, stencil_reach - offset, stencil_reach - offset + extent, axis=direction
            )
            summed = summed + stencil_weights[offset] * (upward + downward)
    return summed


def support_map(atom_coords, starts, extents, periods):
    offsets = jnp.arange(SIDE, dtype=jnp.int32) - SIDE // 2
    clipped_list = []
    inside_list = []
    for index in range(3):
        local = (atom_coords[index][:, None] + offsets[None, :] - starts[index]) % periods[index]
        inside_list.append(local < extents[index])
        clipped_list.append(jnp.minimum(local, extents[index] - 1))
    inside = (
        inside_list[0][:, :, None, None]
        & inside_list[1][:, None, :, None]
        & inside_list[2][:, None, None, :]
    )
    flattened = (
        clipped_list[0][:, :, None, None] * extents[1] + clipped_list[1][:, None, :, None]
    ) * extents[2] + clipped_list[2][:, None, None, :]
    atom_count = atom_coords[0].shape[0]
    return (
        flattened.reshape(atom_count * SUP),
        inside.reshape(atom_count, SUP).astype(jnp.float32),
    )


def coefficients(values, support, inside, projectors):
    orbital_count = values.shape[0]
    atom_count = projectors.shape[0]
    flattened = values.reshape(orbital_count, -1)
    picked = (
        jnp.take(flattened, support, axis=1).reshape(orbital_count, atom_count, SUP) * inside[None]
    )
    partial_coeffs = jnp.einsum("aps,kas->kap", projectors, picked, precision=lax.Precision.HIGHEST)
    return lax.psum(partial_coeffs, "dom")


def spread_into(coeffs, shape, support, inside, projectors, projector_energy):
    orbital_count = shape[0]
    atom_count = projectors.shape[0]
    scaled = coeffs * projector_energy[None, None, :]
    spread = (
        jnp.einsum("aps,kap->kas", projectors, scaled, precision=lax.Precision.HIGHEST)
        * inside[None]
    )
    total_cells = shape[1] * shape[2] * shape[3]
    projected_part = (
        jnp.zeros((orbital_count, total_cells), jnp.float32)
        .at[:, support]
        .add(spread.reshape(orbital_count, atom_count * SUP))
    )
    return projected_part.reshape(shape)


def own_hamiltonian(center, along, local_field, support, inside, projectors, projector_energy):
    kinetic = -0.5 * inverse_spacing * inverse_spacing
    coeffs = coefficients(center, support, inside, projectors)
    projected_part = spread_into(
        coeffs, center.shape, support, inside, projectors, projector_energy
    )
    return kinetic * stencil_sum(center, along) + local_field[None] * center + projected_part


def body(
    orbitals, potential, projectors, projector_energy, atom_first, atom_second, atom_third, rotation
):
    domain_count = lax.axis_size("dom")
    domain_bits = domain_count.bit_length() - 1
    split = [index < domain_bits for index in range(3)]
    start_values = orbitals[0]
    local_field = potential[0]
    extents = start_values.shape[1:]
    periods = (
        extents[0] * min(domain_count, 2),
        extents[1] * min(max(domain_count // 2, 1), 2),
        extents[2] * max(domain_count // 4, 1),
    )
    domain_index = lax.axis_index("dom")
    anchors = (
        domain_index % 2 * extents[0],
        domain_index // 2 % 2 * extents[1],
        domain_index // 4 * extents[2],
    )
    atom_coords = (atom_first, atom_second, atom_third)
    support, inside = support_map(atom_coords, anchors, extents, periods)
    along = [face_padded(start_values, index + 1, index) for index in range(3)]
    first_apply = own_hamiltonian(
        start_values, along, local_field, support, inside, projectors, projector_energy
    )
    first_term = (first_apply - filter_center * start_values) / filter_width
    along = [face_padded(first_term, index + 1, index) for index in range(3)]
    second_apply = own_hamiltonian(
        first_term, along, local_field, support, inside, projectors, projector_energy
    )
    second_term = 2.0 * (second_apply - filter_center * first_term) / filter_width - start_values
    per_device = start_values.shape[0]
    filtered = second_term.astype(jnp.bfloat16).reshape(per_device, -1)
    by_cells = lax.all_to_all(filtered, "orb", split_axis=1, concat_axis=0, tiled=True)
    whole_rotation = lax.all_gather(rotation, "orb", axis=0, tiled=True)
    rotated = lax.dot_general(
        whole_rotation, by_cells, (((0,), (0,)), ((), ())), preferred_element_type=jnp.float32
    ).astype(jnp.bfloat16)
    result = lax.all_to_all(rotated, "orb", split_axis=0, concat_axis=1, tiled=True)
    return result.reshape((1,) + start_values.shape)


def solution(mesh):
    return jax.shard_map(
        body,
        mesh=mesh,
        in_specs=(
            P("dom", "orb", None, None, None),
            P("dom", None, None, None),
            P(),
            P(),
            P(),
            P(),
            P(),
            P("orb", None),
        ),
        out_specs=P("dom", "orb", None, None, None),
        check_vma=False,
    )
```

profile of v0, /device:TPU:33, one launch (start us, length us, event | category | flops | bytes accessed | tf_op | source)
XLA Modules:
  0.0 615.6 jit_solution(15906306912854920774)
XLA Ops:
  3.3 8.8 %collective-permute-start.2 = (bf16[5,12,16,12]{3,2,0,1:T(8,128)(2,1)S(1)}, bf16[5,12,16,12]{3,2,0,1:T(8,128)(2,1)S(1)}, u32[]{:S(2)}, u32[]{:S(2)}) collective-permute-start(bf16[5,12,16,12]{3,2,0,1:T(8,128)(2,1)S(1)} %pad_maximum_fusion.11), channel_id=1, source_target_pairs={{0,256},{256,0},{64,320},{320,64},{128,384},{384,128},{192,448},{4... | collective-permute-start | bytes 69128 | tf_op jit(solution)/shard_map/ppermute | solution.py:33
  13.0 4.9 collective-permute-start.1
  19.5 7.9 %copy.69 = f32[1,5,12,16,128]{1,4,3,2,0:T(8,128)} copy(f32[1,5,12,16,128]{4,3,2,1,0:T(8,128)} %param.14) | data formatting | bytes 983040 | tf_op args[0]
  28.7 32.3 %gather_fusion.1 = f32[8192,5]{1,0:T(8,128)} fusion(f32[5,24576]{0,1:T(8,128)} %bitcast.59, s32[8192]{0:T(1024)S(1)} %fusion.157), kind=kCustom, calls=%fused_computation.1.clone | custom fusion | bytes 360448 | tf_op jit(solution)/shard_map/jit(_take)/gather | solution.py:112
  61.0 7.5 %broadcast_select_fusion.1 = f32[8192,5]{1,0:T(8,128)} fusion(f32[8192,5]{1,0:T(8,128)} %gather_fusion.1, pred[8192]{0:T(1024)(128)(4,1)S(1)} %compare_and_fusion), kind=kLoop, calls=%fused_computation.11 | loop fusion | flops 40960 | bytes 335872 | tf_op jit(solution)/shard_map/jit(_take)/select_n | solution.py:112
  68.5 2.9 copy.71
  72.0 37.3 %psum.14 = f32[5,16,8]{2,0,1:T(8,128)S(1)} all-reduce(f32[5,16,8]{2,0,1:T(8,128)S(1)} %convolution_bitcast_fusion.1), channel_id=1, replica_groups=mesh['dom'=8,'orb'=64] {'dom'}, use_global_device_ids=true, to_apply=%region_0.3 | all-reduce | flops 640 | bytes 5120 | tf_op jit(solution)/shard_map/psum | solution.py:115
  113.1 54.9 %scatter_custom_fusion = f32[5,24576]{0,1:T(8,128)} fusion(s32[8192]{0:T(1024)S(1)} %bitcast.74, f32[8192,5]{1,0:T(8,128)} %copy.73, f32[]{:T(128)} %constant.127.clone.1), kind=kCustom, calls=%fused_computation.8 | custom fusion | flops 40960 | bytes 492032 | tf_op jit(solution)/shard_map/scatter-add | solution.py:130
  168.1 8.3 %copy.74 = f32[5,12,16,128]{3,2,0,1:T(8,128)} copy(f32[5,12,16,128]{0,3,2,1:T(8,128)} %bitcast.56) | data formatting | bytes 983040 | tf_op jit(solution)/shard_map/reshape | solution.py:132
  178.9 6.8 %fusion.168 = (bf16[5,12,16,128]{3,2,0,1:T(8,128)(2,1)S(1)}, f32[5,12,16,128]{3,2,0,1:T(8,128)S(1)}) fusion(f32[5,12,16,128]{3,2,0,1:T(8,128)S(1)} %bitcast.64, f32[5,12,16,128]{3,2,0,1:T(8,128)} %copy.74, f32[12,16,128]{2,1,0:T(8,128)} %bitcast.73, f32[5,12,16,6]{3,2,0,1:T(8,128)} %get-tuple-element.22, f32[5,12,16,6]{3,2,0,1:T(8,128)} %get-tuple-element.21, ...), kind=kLoop, calls=%fused_computation.309 | loop fusion | flops 10690560 | bytes 8131584 | tf_op jit(solution)/shard_map/convert_element_type | solution.py:62
  185.9 8.9 %collective-permute-start.3 = (bf16[5,12,16,128]{3,2,0,1:T(8,128)(2,1)S(1)}, bf16[5,12,16,128]{3,2,0,1:T(8,128)(2,1)}, u32[]{:S(2)}, u32[]{:S(2)}) collective-permute-start(bf16[5,12,16,128]{3,2,0,1:T(8,128)(2,1)S(1)} %get-tuple-element.6), channel_id=1, source_target_pairs={{0,64},{64,0},{128,192},{192,128},{256,320},{320,256},{384,448},{4... | collective-permute-start | bytes 737288 | tf_op jit(solution)/shard_map/ppermute | solution.py:33
  194.9 6.6 %copy.85 = f32[5,12,16,128]{0,3,2,1:T(8,128)} copy(f32[5,12,16,128]{3,2,0,1:T(8,128)S(1)} %broadcast_multiply_fusion) | data formatting | bytes 983040 | tf_op jit(solution)/shard_map/reshape | solution.py:110
  201.5 32.3 %gather_fusion.3 = f32[8192,5]{1,0:T(8,128)} fusion(f32[5,24576]{0,1:T(8,128)} %bitcast.60, s32[8192]{0:T(1024)S(1)} %fusion.157), kind=kCustom, calls=%fused_computation.3.clone | custom fusion | bytes 360448 | tf_op jit(solution)/shard_map/jit(_take)/gather | solution.py:112
  233.8 7.5 %broadcast_select_fusion = f32[8192,5]{1,0:T(8,128)} fusion(f32[8192,5]{1,0:T(8,128)} %gather_fusion.3, pred[8192]{0:T(1024)(128)(4,1)S(1)} %compare_and_fusion), kind=kLoop, calls=%fused_computation.10 | loop fusion | flops 40960 | bytes 335872 | tf_op jit(solution)/shard_map/jit(_take)/select_n | solution.py:112
  241.2 2.8 copy.78
  244.7 36.0 %psum.15 = f32[5,16,8]{2,0,1:T(8,128)S(1)} all-reduce(f32[5,16,8]{2,0,1:T(8,128)S(1)} %convolution_bitcast_fusion), channel_id=1, replica_groups=mesh['dom'=8,'orb'=64] {'dom'}, use_global_device_ids=true, to_apply=%region_2.5 | all-reduce | flops 640 | bytes 5120 | tf_op jit(solution)/shard_map/psum | solution.py:115
  286.6 54.9 %scatter_custom_fusion.1 = f32[5,24576]{0,1:T(8,128)} fusion(s32[8192]{0:T(1024)} %bitcast.75, f32[8192,5]{1,0:T(8,128)} %copy.79, f32[]{:T(128)} %constant.127.clone.1), kind=kCustom, calls=%fused_computation.6 | custom fusion | flops 40960 | bytes 492032 | tf_op jit(solution)/shard_map/scatter-add | solution.py:130
  341.5 7.6 %copy.81 = f32[5,12,16,128]{3,2,0,1:T(8,128)S(1)} copy(f32[5,12,16,128]{0,3,2,1:T(8,128)} %bitcast.55) | data formatting | bytes 983040 | tf_op jit(solution)/shard_map/reshape | solution.py:132
  349.1 8.7 %collective-permute-start.4 = (bf16[5,12,12,128]{3,2,0,1:T(8,128)(2,1)S(1)}, bf16[5,12,12,128]{3,2,0,1:T(8,128)(2,1)S(1)}, u32[]{:S(2)}, u32[]{:S(2)}) collective-permute-start(bf16[5,12,12,128]{3,2,0,1:T(8,128)(2,1)S(1)} %pad_maximum_fusion.12), channel_id=1, source_target_pairs={{0,128},{128,0},{64,192},{192,64},{256,384},{384,256},{320,448},{4... | collective-permute-start | bytes 552968 | tf_op jit(solution)/shard_map/ppermute | solution.py:33
  359.0 4.7 collective-permute-done.4
  368.5 7.5 %subtract_convert_fusion = bf16[5,12,16,128]{3,2,0,1:T(8,128)(2,1)S(1)} fusion(f32[5,12,16,128]{3,2,0,1:T(8,128)S(1)} %get-tuple-element.8, f32[5,12,16,128]{3,2,0,1:T(8,128)S(1)} %copy.81, f32[5,12,16,128]{3,2,0,1:T(8,128)S(1)} %broadcast_multiply_fusion, f32[5,12,16,6]{3,2,0,1:T(8,128)} %get-tuple-element.14, f32[5,12,16,6]{3,2,0,1:T(8,128)} %get-tuple-element.13, ...), kind=kLoop, calls=%fused_computation.265 | loop fusion | flops 10813440 | bytes 8623104 | tf_op jit(solution)/shard_map/convert_element_type | solution.py:177
  377.1 34.7 %all-to-all-start = ((bf16[5,64,384]{2,0,1:T(8,128)(2,1)}), bf16[5,64,384]{2,0,1:T(8,128)(2,1)S(1)}, u32[]{:S(2)}, u32[]{:S(2)}) async-start(bf16[5,64,384]{2,0,1:T(8,128)(2,1)} %copy.83), calls=%async_computation | async-start | bytes 786432 | tf_op jit(solution)/shard_map/all_to_all | solution.py:178
  411.7 163.1 %all-gather = bf16[64,5,320]{2,1,0:T(8,128)(2,1)S(1)} all-gather(bf16[1,5,320]{2,1,0:T(8,128)(2,1)} %bitcast.76), channel_id=1, replica_groups=mesh['dom'=8,'orb'=64] {'orb'}, dimensions={0}, use_global_device_ids=true | all-gather | bytes 208000 | tf_op jit(solution)/shard_map/all_gather | solution.py:179
  575.6 39.2 %all_to_all.35 = bf16[64,5,384]{2,1,0:T(8,128)(2,1)S(1)} all-to-all(bf16[64,5,384]{2,1,0:T(8,128)(2,1)S(1)} %all_to_all.30), channel_id=1, replica_groups=mesh['dom'=8,'orb'=64] {'orb'}, dimensions={0} | all-to-all | bytes 491520 | tf_op jit(solution)/shard_map/all_to_all | solution.py:183
  (79 shorter events, 29.0 us)
Async XLA Ops:
  0.0 71.4 %copy-start = (f32[16,8,512]{2,1,0:T(8,128)S(1)}, f32[16,8,512]{2,1,0:T(8,128)}, u32[]{:S(2)}) copy-start(f32[16,8,512]{2,1,0:T(8,128)} %param.16) | copy-start | bytes 786436
  1.1 177.0 %collective-permute-start = (bf16[5,12,16,128]{3,2,0,1:T(8,128)(2,1)S(1)}, bf16[5,12,16,128]{3,2,0,1:T(8,128)(2,1)S(1)}, u32[]{:S(2)}, u32[]{:S(2)}) collective-permute-start(bf16[5,12,16,128]{3,2,0,1:T(8,128)(2,1)S(1)} %bitcast.65), channel_id=1, source_target_pairs={{0,64},{64,0},{128,192},{192,128},{256,320},{320,256},{384,448},{4... | collective-permute-start | bytes 737288 | tf_op jit(solution)/shard_map/ppermute | solution.py:33
  3.3 173.0 %collective-permute-start.2 = (bf16[5,12,16,12]{3,2,0,1:T(8,128)(2,1)S(1)}, bf16[5,12,16,12]{3,2,0,1:T(8,128)(2,1)S(1)}, u32[]{:S(2)}, u32[]{:S(2)}) collective-permute-start(bf16[5,12,16,12]{3,2,0,1:T(8,128)(2,1)S(1)} %pad_maximum_fusion.11), channel_id=1, source_target_pairs={{0,256},{256,0},{64,320},{320,64},{128,384},{384,128},{192,448},{4... | collective-permute-start | bytes 69128 | tf_op jit(solution)/shard_map/ppermute | solution.py:33
  13.0 164.4 %collective-permute-start.1 = (bf16[5,12,12,128]{3,2,0,1:T(8,128)(2,1)}, bf16[5,12,12,128]{3,2,0,1:T(8,128)(2,1)S(1)}, u32[]{:S(2)}, u32[]{:S(2)}) collective-permute-start(bf16[5,12,12,128]{3,2,0,1:T(8,128)(2,1)} %pad_maximum_fusion.10), channel_id=1, source_target_pairs={{0,128},{128,0},{64,192},{192,64},{256,384},{384,256},{320,448},{4... | collective-permute-start | bytes 552968 | tf_op jit(solution)/shard_map/ppermute | solution.py:33
  28.5 84.6 %copy-start.4 = (s32[8192,1]{0,1:T(1,128)}, s32[8192,1]{0,1:T(1,128)S(1)}, u32[]{:S(2)}) copy-start(s32[8192,1]{0,1:T(1,128)S(1)} %compare_select_fusion) | copy-start | bytes 98308
  68.5 40.9 %copy-start.2 = (f32[1,12,16,128]{3,2,1,0:T(8,128)S(1)}, f32[1,12,16,128]{3,2,1,0:T(8,128)}, u32[]{:S(2)}) copy-start(f32[1,12,16,128]{3,2,1,0:T(8,128)} %param.15) | copy-start | bytes 294916
  68.5 41.6 %copy-start.6 = (f32[8]{0:T(128)S(1)}, f32[8]{0:T(128)}, u32[]{:S(2)}) copy-start(f32[8]{0:T(128)} %param.17) | copy-start | bytes 100
  68.5 41.9 %copy-start.7 = (s32[24]{0:T(128)S(1)}, s32[24]{0:T(128)}, u32[]{:S(2)}) copy-start(s32[24]{0:T(128)} %constant.175) | copy-start | bytes 292
  68.5 42.0 %copy-start.1 = (f32[1,5,12,16,128]{4,3,2,1,0:T(8,128)S(1)}, f32[1,5,12,16,128]{4,3,2,1,0:T(8,128)}, u32[]{:S(2)}) copy-start(f32[1,5,12,16,128]{4,3,2,1,0:T(8,128)} %param.14) | copy-start | bytes 1474564
  110.4 67.8 %copy-start.5 = (s32[1024]{0:T(1024)}, s32[1024]{0:T(1024)S(1)}, u32[]{:S(2)}) copy-start(s32[1024]{0:T(1024)S(1)} %pad_clamp_fusion) | copy-start | bytes 12292
  185.9 178.5 %collective-permute-start.3 = (bf16[5,12,16,128]{3,2,0,1:T(8,128)(2,1)S(1)}, bf16[5,12,16,128]{3,2,0,1:T(8,128)(2,1)}, u32[]{:S(2)}, u32[]{:S(2)}) collective-permute-start(bf16[5,12,16,128]{3,2,0,1:T(8,128)(2,1)S(1)} %get-tuple-element.6), channel_id=1, source_target_pairs={{0,64},{64,0},{128,192},{192,128},{256,320},{320,256},{384,448},{4... | collective-permute-start | bytes 737288 | tf_op jit(solution)/shard_map/ppermute | solution.py:33
  281.9 75.9 %collective-permute-start.5 = (bf16[5,12,16,12]{3,2,0,1:T(8,128)(2,1)}, bf16[5,12,16,12]{3,2,0,1:T(8,128)(2,1)S(1)}, u32[]{:S(2)}, u32[]{:S(2)}) collective-permute-start(bf16[5,12,16,12]{3,2,0,1:T(8,128)(2,1)} %pad_maximum_fusion.13), channel_id=1, source_target_pairs={{0,256},{256,0},{64,320},{320,64},{128,384},{384,128},{192,448},{4... | collective-permute-start | bytes 69128 | tf_op jit(solution)/shard_map/ppermute | solution.py:33
  349.1 14.5 %collective-permute-start.4 = (bf16[5,12,12,128]{3,2,0,1:T(8,128)(2,1)S(1)}, bf16[5,12,12,128]{3,2,0,1:T(8,128)(2,1)S(1)}, u32[]{:S(2)}, u32[]{:S(2)}) collective-permute-start(bf16[5,12,12,128]{3,2,0,1:T(8,128)(2,1)S(1)} %pad_maximum_fusion.12), channel_id=1, source_target_pairs={{0,128},{128,0},{64,192},{192,64},{256,384},{384,256},{320,448},{4... | collective-permute-start | bytes 552968 | tf_op jit(solution)/shard_map/ppermute | solution.py:33
  359.0 9.5 %copy-start.3 = (f32[12,16,128]{2,1,0:T(8,128)S(1)}, f32[12,16,128]{2,1,0:T(8,128)}, u32[]{:S(2)}) copy-start(f32[12,16,128]{2,1,0:T(8,128)} %broadcast_multiply_fusion.1) | copy-start | bytes 294916
  377.1 197.9 %all-to-all-start = ((bf16[5,64,384]{2,0,1:T(8,128)(2,1)}), bf16[5,64,384]{2,0,1:T(8,128)(2,1)S(1)}, u32[]{:S(2)}, u32[]{:S(2)}) async-start(bf16[5,64,384]{2,0,1:T(8,128)(2,1)} %copy.83), calls=%async_computation | async-start | bytes 786432 | tf_op jit(solution)/shard_map/all_to_all | solution.py:178
where the time goes:
time: 618 us; the launch traced here: 616 us
  blocking collectives  276 us (45%)
  other arithmetic  145 us (23%)
  local copies, waits for them, and re-layouts  118 us (19%)
  starting transfers between devices  69.8 us (11%)
    all_gather x1, blocking collectives, body(): whole_rotation = lax.all_gather(rotation, 'orb', axis=0, tiled=True)  163 us
    scatter-add x2, other arithmetic, spread_into(): projected_part = jnp.zeros((orbital_count, total_cells), jnp.float32).at[...  110 us
    psum x2, blocking collectives, coefficients(): return lax.psum(partial_coeffs, 'dom')  73.4 us
    gather x2, local copies, waits for them, and re-layouts, coefficients(): jnp.take(flattened, support, axis=1).reshape(orbital_count, atom_count, SUP)  64.6 us
    all_to_all x1, blocking collectives, body(): lax.all_to_all(rotated, 'orb', split_axis=0, concat_axis=1, tiled=True)  39.2 us
    ppermute x6, starting transfers between devices, partner_2(): return lax.ppermute(block, axis, route)  35.1 us
    all_to_all x1, starting transfers between devices, body(): lax.all_to_all(filtered, 'orb', split_axis=1, concat_axis=0, tiled=True)  34.7 us
    reshape x2, local copies, waits for them, and re-layouts, spread_into(): return projected_part.reshape(shape)  15.9 us
  transfers between devices with their start and end apart: 7, of which 1 were waited for; matrix products, arithmetic and copies ran while one was open for 39% of the time, Pallas kernels for 0%

commit v1 on v0

v1 whole, which is shorter than its diff:
```python
import functools

import jax
import jax.numpy as jnp
import numpy as np
from jax import lax
from jax.experimental import pallas as pl
from jax.experimental.pallas import tpu as pltpu
from jax.sharding import PartitionSpec as P

MESH = pl.DeviceIdType.MESH
F32 = jnp.float32
BF16 = jnp.bfloat16

K, CX, CY, CZ = 5, 12, 16, 128
ROWS = CX * CY
NP = 8
NDOM, NORB_DEV = 8, 64
REACH = 6
WEIGHTS = (
    -5369.0 / 1800.0,
    12.0 / 7.0,
    -15.0 / 56.0,
    10.0 / 189.0,
    -1.0 / 112.0,
    2.0 / 1925.0,
    -1.0 / 16632.0,
)
KINETIC = -8.0
CENTER = 120.0
WIDTH = 110.0


def halves(matrix):
    high = matrix.astype(np.float32).astype(jnp.bfloat16)
    low = (matrix - high.astype(np.float64)).astype(np.float32).astype(jnp.bfloat16)
    return high, low


def hop(distance):
    distance = abs(distance)
    return KINETIC * WEIGHTS[distance] if 1 <= distance <= REACH else 0.0


@functools.cache
def tables():
    own = np.zeros((CX, CY, CX, CY))
    for x in range(CX):
        for y in range(CY):
            for other in range(CX):
                own[x, y, other, y] += hop(x - other)
            for other in range(CY):
                own[x, y, x, other] += hop(y - other)
    own_high, own_low = halves(own.reshape(ROWS, ROWS))
    own3 = np.concatenate((own_high, own_low, own_high), axis=1)

    near = np.zeros((CX, CY, CX, CY))
    for x in range(CX):
        for other in range(CX):
            near[x, np.arange(CY), other, np.arange(CY)] = hop(other + CX - x) + hop(other - CX - x)
    kept = list(range(REACH)) + list(range(CY - REACH, CY))
    side = np.zeros((CX, CY, CX, 2 * REACH))
    pick_y = np.zeros((CX, 2 * REACH, CX, CY))
    for slot, row in enumerate(kept):
        for x in range(CX):
            pick_y[x, slot, x, row] = 1.0
            for y in range(CY):
                side[x, y, x, slot] = hop(row + CY - y) + hop(row - CY - y)
    both = np.concatenate((near.reshape(ROWS, ROWS), side.reshape(ROWS, 12 * CX)), axis=1)
    both_high, both_low = halves(both)
    both2 = np.concatenate((both_high, both_low), axis=1)
    pick_y = pick_y.reshape(12 * CX, ROWS).astype(jnp.bfloat16)

    line = np.array([[hop(z - other) for other in range(CZ)] for z in range(CZ)])
    line_high, line_low = halves(line)
    line3 = np.concatenate((line_high, line_high, line_low), axis=0)

    pick_z = np.zeros((6, CZ, CZ))
    ends = np.zeros((CZ, 6, CZ))
    lanes = list(range(REACH)) + list(range(CZ - REACH, CZ))
    for g in range(6):
        for slot, lane in enumerate(lanes):
            pick_z[g, lane, 12 * g + slot] = 1.0
            for z in range(CZ):
                ends[12 * g + slot, g, z] = hop(lane + CZ - z) + hop(lane - CZ - z)
    ends_high, ends_low = halves(ends.reshape(CZ, 6 * CZ))
    ends2 = np.concatenate((ends_high, ends_low), axis=0)
    pick_z = pick_z.reshape(6 * CZ, CZ).astype(jnp.bfloat16)

    to_tiles = np.zeros((16, 16, 15, 16))
    for q in range(16):
        for m in range(15):
            to_tiles[q, m, m, q] = 1.0
    to_tiles = to_tiles.reshape(256, 240).astype(jnp.bfloat16)
    from_tiles = np.ascontiguousarray(to_tiles.T)

    widen = np.zeros((16, 16, 16, 16))
    for s in range(16):
        for c in range(3):
            for o in range(K):
                for r in range(3):
                    widen[s, 5 * c + o, s, 3 * o + r] = 1.0
    widen = widen.reshape(256, 256).astype(jnp.bfloat16)
    return own3, both2, line3, ends2, pick_y, pick_z, to_tiles, from_tiles, widen


def split(values):
    high = values.astype(BF16)
    low = (values - high.astype(F32)).astype(BF16)
    return high, low


def dot(a, b):
    return jnp.dot(a, b, preferred_element_type=F32)


def exact_dot(a, b):
    return jnp.dot(a, b, preferred_element_type=F32, precision=lax.Precision.HIGHEST)


def kernel(
    first_s, second_s, third_s, energy_s,
    x_ref, v_ref, proj_ref, rot_ref,
    own3, both2, line3, ends2, pick_y, pick_z, to_tiles, from_tiles, widen,
    out_ref,
    turned, across, pxy, szf, y1, acc,
    xsend, ysend, zsend, xrecv, yrecv, zrecv,
    cmsg, crecv, cfull,
    rtmp, rtile, rring, rother, rall,
    rbig, fb, fsend, frecv, gsend, grecv,
    halo_ssem, halo_rsem, c_ssem, c_rsem, ring_ssem, ring_rsem, hand_ssem, hand_rsem, r_ssem, r_rsem, t_ssem, t_rsem,
):
    dom = lax.axis_index("dom")
    orb = lax.axis_index("orb")
    zhi = (orb // 2) % 2
    lane_u = (orb // 4) * 2 + orb % 2

    def plane_peer(i):
        u = (lane_u + i) % 32
        return (dom, (u // 2) * 4 + zhi * 2 + u % 2)

    def dom_peer(i):
        return ((dom + i) % NDOM, orb)

    def ring_peer(step):
        z = (zhi * 8 + dom + step + 16) % 16
        return (z % 8, orb - zhi * 2 + (z // 8) * 2)

    partners = (
        (dom + 1 - 2 * (dom % 2), orb),
        (dom + 2 - 4 * ((dom // 2) % 2), orb),
        (dom + 4 - 8 * (dom // 4), orb),
    )

    barrier = pltpu.get_barrier_semaphore()

    def greet_plane(i, carry):
        pl.semaphore_signal(barrier, inc=1, device_id=plane_peer(i), device_id_type=MESH)
        return carry

    def greet_dom(i, carry):
        pl.semaphore_signal(barrier, inc=1, device_id=dom_peer(i), device_id_type=MESH)
        return carry

    lax.fori_loop(1, NDOM, greet_dom, 0)
    for step in (1, -1):
        pl.semaphore_signal(barrier, inc=1, device_id=ring_peer(step), device_id_type=MESH)
    lax.fori_loop(1, 32, greet_plane, 0)

    lane = lax.broadcasted_iota(jnp.int32, (8, 128), 1)
    sub = lax.broadcasted_iota(jnp.int32, (8, 128), 0)
    first = jnp.zeros((8, 128), jnp.int32)
    second = first
    third = first
    for a in range(16):
        mine = lane // 8 == a
        first = jnp.where(mine, first_s[a], first)
        second = jnp.where(mine, second_s[a], second)
        third = jnp.where(mine, third_s[a], third)
    energy = jnp.zeros((8, 128), F32)
    for p in range(NP):
        energy = jnp.where(sub == p, energy_s[p], energy)
    shift_x = (first - 4 - (dom % 2) * CX + 48) % 24
    shift_y = (second - 4 - (dom // 2 % 2) * CY + 64) % 32
    start_z = (third - 4 - (dom // 4) * CZ + 512) % 256
    cell_z = (start_z + lane % 8) % 256

    swapped = proj_ref[...].T.reshape(64, 8, 128)
    lane3 = lax.broadcasted_iota(jnp.int32, (64, 8, 128), 2)
    sub3 = lax.broadcasted_iota(jnp.int32, (64, 8, 128), 1)
    for bit in (1, 2, 4):
        up = pltpu.roll(pltpu.roll(swapped, 8 - bit, 1), bit, 2)
        down = pltpu.roll(pltpu.roll(swapped, bit, 1), 128 - bit, 2)
        low_s = (sub3 // bit) % 2 == 0
        low_l = (lane3 // bit) % 2 == 0
        swapped = jnp.where(
            jnp.logical_and(low_s, jnp.logical_not(low_l)),
            up,
            jnp.where(jnp.logical_and(jnp.logical_not(low_s), low_l), down, swapped),
        )
    turned[...] = swapped.reshape(512, 128)

    fine = shift_y % 8
    tile_of = jnp.where(sub >= fine, shift_y // 8, (shift_y // 8 + 1) % 4)

    def place_y(i, carry):
        for p in range(NP):
            rows = turned[pl.ds(i * 64 + p, 8, stride=8), :]
            for bit in (1, 2, 4):
                rows = jnp.where((fine // bit) % 2 == 1, pltpu.roll(rows, bit, 0), rows)
            for half_y in range(2):
                across[i, p, pl.ds(8 * half_y, 8), :] = jnp.where(tile_of == half_y, rows, 0.0)
        return carry

    lax.fori_loop(0, 8, place_y, 0)

    def place_x(x, carry):
        hits = [shift_x == (x - i + 24) % 24 for i in range(8)]
        for p in range(NP):
            for half_y in range(2):
                total = jnp.zeros((8, 128), F32)
                for i in range(8):
                    total = jnp.where(hits[i], across[i, p, pl.ds(8 * half_y, 8), :], total)
                pxy[p, pl.ds(x * 16 + 8 * half_y, 8), :] = total
        return carry

    lax.fori_loop(0, CX, place_x, 0)

    zrow = lax.broadcasted_iota(jnp.int32, (128, 128), 0)
    onehot = jnp.where(zrow == jnp.broadcast_to(cell_z[0:1, :], (128, 128)), 1.0, 0.0)
    szf[0] = onehot.astype(BF16)
    szf[1] = onehot.T.astype(BF16)

    lane_128 = lax.broadcasted_iota(jnp.int32, (128, 128), 1)

    def partial_coefficients(source, slot):
        packed = jnp.zeros((8, 128), F32)
        for k in range(K):
            high, low = split(source[k])
            picked = dot(high, szf[0]) + dot(low, szf[0])
            sums = [jnp.sum(picked * pxy[p], axis=0, keepdims=True) for p in range(NP)]
            own = jnp.concatenate(sums, axis=0)
            gather = jnp.where(zrow // 8 + 16 * k == lane_128, 1.0, 0.0)
            packed = packed + exact_dot(own, gather)
        cmsg[slot] = packed
        crecv[slot, dom] = packed

    def send_coefficients(slot):
        copies = []
        for i in range(1, NDOM):
            copies.append(
                pltpu.make_async_remote_copy(
                    src_ref=cmsg.at[slot],
                    dst_ref=crecv.at[slot, dom],
                    send_sem=c_ssem.at[slot],
                    recv_sem=c_rsem.at[slot],
                    device_id=dom_peer(i),
                    device_id_type=MESH,
                )
            )
            copies[-1].start()

    def await_coefficients(slot):
        every = pltpu.make_async_remote_copy(
            src_ref=crecv.at[slot, pl.ds(0, NDOM - 1)],
            dst_ref=crecv.at[slot, pl.ds(0, NDOM - 1)],
            send_sem=c_ssem.at[slot],
            recv_sem=c_rsem.at[slot],
            device_id=dom_peer(1),
            device_id_type=MESH,
        )
        every.wait()
        total = crecv[slot, 0]
        for i in range(1, NDOM):
            total = total + crecv[slot, i]
        total = total * energy
        for k in range(K):
            gather = jnp.where(zrow == lane_128 // 8 + 16 * k, 1.0, 0.0)
            cfull[k] = exact_dot(total, gather)

    def pack_halo(values, level, k):
        high = values.astype(BF16)
        xsend[level, k] = high
        ysend[level, k] = dot(pick_y[...], high).astype(BF16)
        packed = dot(high[0:32], pick_z[0:128, :])
        for g in range(1, 6):
            packed = packed + dot(high[32 * g : 32 * g + 32], pick_z[128 * g : 128 * g + 128, :])
        zsend[level, k] = packed.astype(BF16)

    def halo_copies(level, k):
        pairs = ((zsend, zrecv, 2), (ysend, yrecv, 1), (xsend, xrecv, 0))
        return [
            pltpu.make_async_remote_copy(
                src_ref=source.at[level, k],
                dst_ref=target.at[level, k],
                send_sem=halo_ssem.at[level, axis, k],
                recv_sem=halo_rsem.at[level, axis, k],
                device_id=partners[axis],
                device_id_type=MESH,
            )
            for source, target, axis in pairs
        ]

    def own_part(source, k):
        values = source[k]
        high, low = split(values)
        total = dot(own3[...], jnp.concatenate((high, high, low), axis=0))
        total = total + dot(jnp.concatenate((high, low, high), axis=1), line3[...])
        local = v_ref[...] + (3.0 * KINETIC * WEIGHTS[0] - CENTER)
        acc[k] = total + local * values

    def nonlocal_part(k):
        spread = pxy[0] * cfull[k, 0:1, :]
        for p in range(1, NP):
            spread = spread + pxy[p] * cfull[k, p : p + 1, :]
        high, low = split(spread)
        acc[k] = acc[k] + dot(high, szf[1]) + dot(low, szf[1])

    def halo_part(level, k):
        for copy in halo_copies(level, k):
            copy.wait_recv()
        got = jnp.concatenate((xrecv[level, k], yrecv[level, k]), axis=0)
        total = acc[k] + dot(both2[...], jnp.concatenate((got, got), axis=0))
        zgot = zrecv[level, k]
        ends = dot(jnp.concatenate((zgot, zgot), axis=1), ends2[...])
        flat = jnp.concatenate([ends[:, 128 * g : 128 * g + 128] for g in range(6)], axis=0)
        return total + flat

    partial_coefficients(x_ref, 0)
    for k in range(K):
        pack_halo(x_ref[k], 0, k)
    rtmp[...] = jnp.zeros((16, 128), F32)
    wide = rot_ref[...].astype(F32)
    rtmp[0:5, :] = wide[:, 0:128]
    rtmp[5:10, :] = wide[:, 128:256]
    rtmp[10:15, 0:64] = wide[:, 256:320]
    rtile[...] = rtmp[...].astype(BF16)
    rall[orb] = rtile[...]

    pl.semaphore_wait(barrier, 31 + 7 + 2)
    send_coefficients(0)
    for k in range(K):
        for copy in halo_copies(0, k):
            copy.start()

    def tile_copy(source, i, slot, wave):
        return pltpu.make_async_remote_copy(
            src_ref=source,
            dst_ref=rall.at[slot],
            send_sem=r_ssem.at[wave],
            recv_sem=r_rsem.at[wave],
            device_id=plane_peer(i),
            device_id_type=MESH,
        )

    def send_rows(i, carry):
        tile_copy(rtile, i, orb, 0).start()
        return carry

    lax.fori_loop(1, 32, send_rows, 0)

    for k in range(K):
        own_part(x_ref, k)

    await_coefficients(0)
    ring_copies = []
    for index, step in enumerate((1, -1)):
        ring_copies.append(
            pltpu.make_async_remote_copy(
                src_ref=rtile,
                dst_ref=rring.at[index],
                send_sem=ring_ssem.at[index],
                recv_sem=ring_rsem.at[index],
                device_id=ring_peer(step),
                device_id_type=MESH,
            )
        )
        ring_copies[-1].start()

    for k in range(K):
        nonlocal_part(k)
    for k in range(K):
        y1[k] = halo_part(0, k) * (1.0 / WIDTH)
        pack_halo(y1[k], 1, k)
        if k < 3:
            for copy in halo_copies(1, k):
                copy.start()

    partial_coefficients(y1, 1)
    for copy in ring_copies:
        copy.wait()
    send_coefficients(1)
    hands = [
        pltpu.make_async_remote_copy(
            src_ref=rring.at[1],
            dst_ref=rother,
            send_sem=hand_ssem.at[i],
            recv_sem=hand_rsem,
            device_id=dom_peer(i + 1),
            device_id_type=MESH,
        )
        for i in range(NDOM - 1)
    ]

    @pl.when(dom == NDOM - 1)
    def _():
        for copy in hands:
            copy.start()
        rother[...] = rring[1]

    for k in range(3, K):
        for copy in halo_copies(1, k):
            copy.start()

    for k in range(K):
        own_part(y1, k)

    @pl.when(dom == NDOM - 1)
    def _():
        for copy in hands:
            copy.wait_send()

    @pl.when(dom != NDOM - 1)
    def _():
        hands[0].wait_recv()

    orb_other = orb + 2 - 4 * zhi
    rall[orb_other] = rother[...]

    await_coefficients(1)

    def send_other(i, carry):
        tile_copy(rother, i, orb_other, 1).start()
        return carry

    lax.fori_loop(1, 32, send_other, 0)

    for k in range(K):
        nonlocal_part(k)
    for level in range(2):
        for k in range(K):
            for copy in halo_copies(level, k):
                copy.wait_send()
    for k in range(K):
        fb[k] = (halo_part(1, k) * (2.0 / WIDTH) - x_ref[k]).astype(BF16)
    for g in range(4):
        rows = [fb[o, pl.ds((4 * r + g) * 16, 16), :] for o in range(K) for r in range(3)]
        tiles = dot(to_tiles[...], jnp.concatenate(rows, axis=0))
        fsend[16 * g : 16 * g + 16] = tiles.astype(BF16).reshape(16, 16, 128)

    def exchange(source, target, q, wave):
        return pltpu.make_async_remote_copy(
            src_ref=source,
            dst_ref=target,
            send_sem=t_ssem.at[wave],
            recv_sem=t_rsem.at[wave],
            device_id=(dom, q),
            device_id_type=MESH,
        )

    def send_cells(i, carry):
        q = (orb + i) % NORB_DEV
        exchange(fsend.at[q], frecv.at[orb], q, 0).start()
        return carry

    lax.fori_loop(1, NORB_DEV, send_cells, 0)
    frecv[orb] = fsend[orb]

    for wave in range(2):
        every = tile_copy(rall.at[pl.ds(0, 31)], 1, pl.ds(0, 31), wave)
        every.wait()
    rows_all = rall[...].reshape(1024, 128)
    row_e = lax.broadcasted_iota(jnp.int32, (256, 128), 0)
    lane_e = lax.broadcasted_iota(jnp.int32, (256, 128), 1)
    col_a = lax.broadcasted_iota(jnp.int32, (256, 1024), 1)
    row_b = lax.broadcasted_iota(jnp.int32, (256, 256), 0) % 16
    col_b = lax.broadcasted_iota(jnp.int32, (256, 256), 1) % 16
    same = row_b - 3 * (row_b * 11 // 32) == col_b - 3 * (col_b * 11 // 32)
    third_of = (col_a % 16) * 13 // 64

    def widen_rows(chunk, carry):
        member = row_e % 16
        target = 5 * (chunk * 16 + row_e // 16) + member * 11 // 32
        target = jnp.where(member < 15, target, -1000)
        mixed = jnp.zeros((256, 1024), F32)
        for c in range(3):
            pick = jnp.where(lane_e == target - 128 * c, 1.0, 0.0).astype(BF16)
            part = lax.dot_general(
                pick, rows_all, (((1,), (1,)), ((), ())), preferred_element_type=F32
            )
            mixed = jnp.where(third_of == c, part, mixed)
        mixed = mixed.astype(BF16)
        for s in range(4):
            block = dot(mixed[:, 256 * s : 256 * s + 256], widen[...])
            rbig[pl.ds(chunk * 256, 256), pl.ds(256 * s, 256)] = jnp.where(same, block, 0.0).astype(BF16)
        return carry

    lax.fori_loop(0, 4, widen_rows, 0)

    every = exchange(fsend.at[pl.ds(0, 63)], frecv.at[pl.ds(0, 63)], orb, 0)
    every.wait()
    cells = frecv[...].reshape(1024, 128)
    for i in range(4):
        chunk = (orb // 16 + i) % 4
        turned_cells = dot(rbig[pl.ds(pl.multiple_of(chunk * 256, 256), 256), :], cells)
        gsend[pl.ds(chunk * 16, 16)] = turned_cells.astype(BF16).reshape(16, 16, 128)

        def send_back(j, carry):
            q = chunk * 16 + (orb % 16 + j) % 16
            exchange(gsend.at[q], grecv.at[orb], q, 1).start()
            return carry

        lax.fori_loop(1 if i == 0 else 0, 16, send_back, 0)
    grecv[orb] = gsend[orb]
    every = exchange(gsend.at[pl.ds(0, 63)], grecv.at[pl.ds(0, 63)], orb, 1)
    every.wait()
    for g in range(4):
        rows = dot(from_tiles[...], grecv[16 * g : 16 * g + 16].reshape(256, 128)).astype(BF16)
        for o in range(K):
            for r in range(3):
                m = 3 * o + r
                out_ref[o, pl.ds((4 * r + g) * 16, 16), :] = rows[16 * m : 16 * m + 16]


def body(
    orbitals, potential, projectors, projector_energy, atom_first, atom_second, atom_third, rotation
):
    consts = [jnp.asarray(t) for t in tables()]
    smem = pl.BlockSpec(memory_space=pltpu.SMEM)
    vmem = pl.BlockSpec(memory_space=pltpu.VMEM)
    dma = pltpu.SemaphoreType.DMA
    scratch = [
        pltpu.VMEM((512, 128), F32),
        pltpu.VMEM((8, NP, 16, 128), F32),
        pltpu.VMEM((NP, ROWS, 128), F32),
        pltpu.VMEM((2, 128, 128), BF16),
        pltpu.VMEM((K, ROWS, CZ), F32),
        pltpu.VMEM((K, ROWS, CZ), F32),
        pltpu.VMEM((2, K, ROWS, CZ), BF16),
        pltpu.VMEM((2, K, 144, CZ), BF16),
        pltpu.VMEM((2, K, 32, CZ), BF16),
        pltpu.VMEM((2, K, ROWS, CZ), BF16),
        pltpu.VMEM((2, K, 144, CZ), BF16),
        pltpu.VMEM((2, K, 32, CZ), BF16),
        pltpu.VMEM((2, 8, 128), F32),
        pltpu.VMEM((2, NDOM, 8, 128), F32),
        pltpu.VMEM((K, 8, 128), F32),
        pltpu.VMEM((16, 128), F32),
        pltpu.VMEM((16, 128), BF16),
        pltpu.VMEM((2, 16, 128), BF16),
        pltpu.VMEM((16, 128), BF16),
        pltpu.VMEM((NORB_DEV, 16, 128), BF16),
        pltpu.VMEM((1024, 1024), BF16),
        pltpu.VMEM((K, ROWS, CZ), BF16),
        pltpu.VMEM((NORB_DEV, 16, 128), BF16),
        pltpu.VMEM((NORB_DEV, 16, 128), BF16),
        pltpu.VMEM((NORB_DEV, 16, 128), BF16),
        pltpu.VMEM((NORB_DEV, 16, 128), BF16),
        dma((2, 3, K)),
        dma((2, 3, K)),
        dma((2,)),
        dma((2,)),
        dma((2,)),
        dma((2,)),
        dma((NDOM - 1,)),
        dma(()),
        dma((2,)),
        dma((2,)),
        dma((2,)),
        dma((2,)),
    ]
    result = pl.pallas_call(
        kernel,
        out_shape=jax.ShapeDtypeStruct((K, ROWS, CZ), BF16),
        in_specs=[smem] * 4 + [vmem] * (4 + len(consts)),
        out_specs=vmem,
        scratch_shapes=scratch,
        compiler_params=pltpu.CompilerParams(
            collective_id=0, has_side_effects=True, vmem_limit_bytes=60 << 20
        ),
        name="filter_rotate",
    )(
        atom_first,
        atom_second,
        atom_third,
        projector_energy,
        orbitals.reshape(K, ROWS, CZ),
        potential.reshape(ROWS, CZ),
        projectors.reshape(128, 512),
        rotation,
        *consts,
    )
    return result.reshape((1, K, CX, CY, CZ))


def solution(mesh):
    return jax.shard_map(
        body,
        mesh=mesh,
        in_specs=(
            P("dom", "orb", None, None, None),
            P("dom", None, None, None),
            P(),
            P(),
            P(),
            P(),
            P(),
            P("orb", None),
        ),
        out_specs=P("dom", "orb", None, None, None),
        check_vma=False,
    )
```

time: 618 us -> 83.7 us (0.14)
  blocking collectives: 276 us -> 0 us
  other arithmetic: 145 us -> 0 us
  local copies, waits for them, and re-layouts: 118 us -> 1.65 us
  Pallas kernels: 0 us -> 81.8 us
  starting transfers between devices: 69.8 us -> 0 us
    all_gather x1 -> x0, blocking collectives: 163 us -> none  [body(): whole_rotation = lax.all_gather(rotation, 'orb', axis=0, tiled=True)]
    scatter-add x2 -> x0, other arithmetic: 110 us -> none  [spread_into(): projected_part = jnp.zeros((orbital_count, total_cells), jnp.float32).at[...]
    pallas_call x0 -> x1, Pallas kernels: none -> 81.8 us  [body(): pl.pallas_call(kernel, out_shape=jax.ShapeDtypeStruct((K, ROWS, CZ), BF16...]
    psum x2 -> x0, blocking collectives: 73.4 us -> none  [coefficients(): return lax.psum(partial_coeffs, 'dom')]
    gather x4 -> x0, local copies, waits for them, and re-layouts: 67.2 us -> none  [the longest x2 64.6 us: coefficients(): jnp.take(flattened, support, axis=1).reshape(orbital_count, atom_count, SUP)]
    all_to_all x1 -> x0, blocking collectives: 39.2 us -> none  [body(): lax.all_to_all(rotated, 'orb', split_axis=0, concat_axis=1, tiled=True)]
    ppermute x6 -> x0, starting transfers between devices: 35.1 us -> none  [partner_2(): return lax.ppermute(block, axis, route)]
    all_to_all x1 -> x0, starting transfers between devices: 34.7 us -> none  [body(): lax.all_to_all(filtered, 'orb', split_axis=1, concat_axis=0, tiled=True)]
  transfers between devices with their start and end apart: 7 -> 0, of which waited for: 1 -> 0; matrix products, arithmetic and copies ran while one was open for 39% -> 0% of each run, Pallas kernels for 0% -> 0%
where the time goes in v1:
time: 83.7 us; the launch traced here: 83.5 us
  Pallas kernels  81.8 us (98%)
  local copies, waits for them, and re-layouts  1.65 us (2%)
    pallas_call x1, Pallas kernels, body(): pl.pallas_call(kernel, out_shape=jax.ShapeDtypeStruct((K, ROWS, CZ), BF16...  81.8 us

profile of v1, /device:TPU:33, one launch (start us, length us, event | category | flops | bytes accessed | tf_op | source)
XLA Modules:
  0.0 83.5 jit_solution(17413549863181960386)
XLA Ops:
  0.0 81.8 %filter_rotate.1 = bf16[5,192,128]{2,1,0:T(8,128)(2,1)} custom-call(s32[16]{0:T(128)} %first_s.1, s32[16]{0:T(128)} %second_s.1, s32[16]{0:T(128)} %third_s.1, f32[8]{0:T(128)} %energy_s.1, f32[5,192,128]{2,1,0:T(8,128)} %bitcast.5, f32[192,128]{1,0:T(8,128)} %bitcast.7, f32[128,512]{1,0:T(8,128)} %bitcast.6, bf16[5,320]{1,0:T(8,128)(2,1)} %rot_ref.1, ...), custom_call_target="tpu_custom_call" | custom-call | tf_op jit(solution)/shard_map/filter_rotate/pallas_call | solution.py:572
  81.9 1.7 %copy.19 = bf16[1,5,12,16,128]{4,3,2,1,0:T(8,128)(2,1)} copy(bf16[1,5,12,16,128]{4,3,2,1,0:T(8,128)(2,1)} %bitcast.4) | data formatting | bytes 491520

commit v2 on v1

--- a/solution.py
+++ b/solution.py
@@ -17,6 +17,7 @@
 NP = 8
 NDOM, NORB_DEV = 8, 64
 REACH = 6
+AHEAD = 2
 WEIGHTS = (
     -5369.0 / 1800.0,
     12.0 / 7.0,
@@ -120,15 +121,16 @@
 
 def kernel(
     first_s, second_s, third_s, energy_s,
-    x_ref, v_ref, proj_ref, rot_ref,
-    own3, both2, line3, ends2, pick_y, pick_z, to_tiles, from_tiles, widen,
+    x_hbm, v_hbm, proj_hbm, rot_ref,
+    own3_hbm, both2_hbm, line3_hbm, ends2_hbm, pick_y_hbm, pick_z_hbm, to_tiles_hbm, from_tiles_hbm, widen_hbm,
     out_ref,
+    x_ref, v_ref, proj_ref, own3, both2, line3, ends2, pick_y, pick_z, to_tiles, from_tiles, widen,
     turned, across, pxy, szf, y1, acc,
     xsend, ysend, zsend, xrecv, yrecv, zrecv,
     cmsg, crecv, cfull,
     rtmp, rtile, rring, rother, rall,
     rbig, fb, fsend, frecv, gsend, grecv,
-    halo_ssem, halo_rsem, c_ssem, c_rsem, ring_ssem, ring_rsem, hand_ssem, hand_rsem, r_ssem, r_rsem, t_ssem, t_rsem,
+    halo_ssem, halo_rsem, c_ssem, c_rsem, ring_ssem, ring_rsem, hand_ssem, hand_rsem, r_ssem, r_rsem, t_ssem, t_rsem, in_sem,
 ):
     dom = lax.axis_index("dom")
     orb = lax.axis_index("orb")
@@ -166,6 +168,28 @@
     for step in (1, -1):
         pl.semaphore_signal(barrier, inc=1, device_id=ring_peer(step), device_id_type=MESH)
     lax.fori_loop(1, 32, greet_plane, 0)
+
+    inputs = [
+        pltpu.make_async_copy(source, target, in_sem.at[index])
+        for index, (source, target) in enumerate(
+            (
+                (proj_hbm, proj_ref),
+                (x_hbm, x_ref),
+                (pick_y_hbm, pick_y),
+                (pick_z_hbm, pick_z),
+                (own3_hbm, own3),
+                (line3_hbm, line3),
+                (v_hbm, v_ref),
+                (both2_hbm, both2),
+                (ends2_hbm, ends2),
+                (widen_hbm, widen),
+                (to_tiles_hbm, to_tiles),
+                (from_tiles_hbm, from_tiles),
+            )
+        )
+    ]
+    for copy in inputs:
+        copy.start()
 
     lane = lax.broadcasted_iota(jnp.int32, (8, 128), 1)
     sub = lax.broadcasted_iota(jnp.int32, (8, 128), 0)
@@ -185,6 +209,7 @@
     start_z = (third - 4 - (dom // 4) * CZ + 512) % 256
     cell_z = (start_z + lane % 8) % 256
 
+    inputs[0].wait()
     swapped = proj_ref[...].T.reshape(64, 8, 128)
     lane3 = lax.broadcasted_iota(jnp.int32, (64, 8, 128), 2)
     sub3 = lax.broadcasted_iota(jnp.int32, (64, 8, 128), 1)
@@ -233,15 +258,15 @@
 
     lane_128 = lax.broadcasted_iota(jnp.int32, (128, 128), 1)
 
-    def partial_coefficients(source, slot):
-        packed = jnp.zeros((8, 128), F32)
-        for k in range(K):
-            high, low = split(source[k])
-            picked = dot(high, szf[0]) + dot(low, szf[0])
-            sums = [jnp.sum(picked * pxy[p], axis=0, keepdims=True) for p in range(NP)]
-            own = jnp.concatenate(sums, axis=0)
-            gather = jnp.where(zrow // 8 + 16 * k == lane_128, 1.0, 0.0)
-            packed = packed + exact_dot(own, gather)
+    def partial_coefficients(source, k):
+        high, low = split(source[k])
+        picked = dot(high, szf[0]) + dot(low, szf[0])
+        sums = [jnp.sum(picked * pxy[p], axis=0, keepdims=True) for p in range(NP)]
+        own = jnp.concatenate(sums, axis=0)
+        gather = jnp.where(zrow // 8 + 16 * k == lane_128, 1.0, 0.0)
+        return exact_dot(own, gather)
+
+    def hold_coefficients(packed, slot):
         cmsg[slot] = packed
         crecv[slot, dom] = packed
 
@@ -326,7 +351,13 @@
         flat = jnp.concatenate([ends[:, 128 * g : 128 * g + 128] for g in range(6)], axis=0)
         return total + flat
 
-    partial_coefficients(x_ref, 0)
+    inputs[1].wait()
+    packed = jnp.zeros((8, 128), F32)
+    for k in range(K):
+        packed = packed + partial_coefficients(x_ref, k)
+    hold_coefficients(packed, 0)
+    inputs[2].wait()
+    inputs[3].wait()
     for k in range(K):
         pack_halo(x_ref[k], 0, k)
     rtmp[...] = jnp.zeros((16, 128), F32)
@@ -359,6 +390,8 @@
 
     lax.fori_loop(1, 32, send_rows, 0)
 
+    for copy in inputs[4:]:
+        copy.wait()
     for k in range(K):
         own_part(x_ref, k)
 
@@ -377,19 +410,6 @@
         )
         ring_copies[-1].start()
 
-    for k in range(K):
-        nonlocal_part(k)
-    for k in range(K):
-        y1[k] = halo_part(0, k) * (1.0 / WIDTH)
-        pack_halo(y1[k], 1, k)
-        if k < 3:
-            for copy in halo_copies(1, k):
-                copy.start()
-
-    partial_coefficients(y1, 1)
-    for copy in ring_copies:
-        copy.wait()
-    send_coefficients(1)
     hands = [
         pltpu.make_async_remote_copy(
             src_ref=rring.at[1],
@@ -401,14 +421,28 @@
         )
         for i in range(NDOM - 1)
     ]
-
-    @pl.when(dom == NDOM - 1)
-    def _():
-        for copy in hands:
-            copy.start()
-        rother[...] = rring[1]
-
-    for k in range(3, K):
+    packed = jnp.zeros((8, 128), F32)
+    for k in range(K):
+        nonlocal_part(k)
+        y1[k] = halo_part(0, k) * (1.0 / WIDTH)
+        pack_halo(y1[k], 1, k)
+        if k < AHEAD:
+            for copy in halo_copies(1, k):
+                copy.start()
+        packed = packed + partial_coefficients(y1, k)
+        if k == AHEAD - 1:
+            for copy in ring_copies:
+                copy.wait()
+
+            @pl.when(dom == NDOM - 1)
+            def _():
+                for copy in hands:
+                    copy.start()
+                rother[...] = rring[1]
+
+    hold_coefficients(packed, 1)
+    send_coefficients(1)
+    for k in range(AHEAD, K):
         for copy in halo_copies(1, k):
             copy.start()
 
@@ -427,13 +461,13 @@
     orb_other = orb + 2 - 4 * zhi
     rall[orb_other] = rother[...]
 
-    await_coefficients(1)
 
     def send_other(i, carry):
         tile_copy(rother, i, orb_other, 1).start()
         return carry
 
     lax.fori_loop(1, 32, send_other, 0)
+    await_coefficients(1)
 
     for k in range(K):
         nonlocal_part(k)
@@ -458,12 +492,18 @@
             device_id_type=MESH,
         )
 
-    def send_cells(i, carry):
-        q = (orb + i) % NORB_DEV
-        exchange(fsend.at[q], frecv.at[orb], q, 0).start()
-        return carry
-
-    lax.fori_loop(1, NORB_DEV, send_cells, 0)
+    core = orb % 2
+    groups = (2 - 2 * zhi + core, 3 - 2 * zhi - core, 2 * zhi + 1 - core, 2 * zhi + core)
+    place = orb // 4
+
+    for index, group in enumerate(groups):
+
+        def send_cells(j, carry):
+            q = (place + j) % 16 * 4 + group
+            exchange(fsend.at[q], frecv.at[orb], q, 0).start()
+            return carry
+
+        lax.fori_loop(1 if index == 3 else 0, 16, send_cells, 0)
     frecv[orb] = fsend[orb]
 
     for wave in range(2):
@@ -480,7 +520,7 @@
 
     def widen_rows(chunk, carry):
         member = row_e % 16
-        target = 5 * (chunk * 16 + row_e // 16) + member * 11 // 32
+        target = 5 * (row_e // 16 * 4 + chunk) + member * 11 // 32
         target = jnp.where(member < 15, target, -1000)
         mixed = jnp.zeros((256, 1024), F32)
         for c in range(3):
@@ -500,18 +540,18 @@
     every = exchange(fsend.at[pl.ds(0, 63)], frecv.at[pl.ds(0, 63)], orb, 0)
     every.wait()
     cells = frecv[...].reshape(1024, 128)
-    for i in range(4):
-        chunk = (orb // 16 + i) % 4
+    for index, chunk in enumerate(groups):
         turned_cells = dot(rbig[pl.ds(pl.multiple_of(chunk * 256, 256), 256), :], cells)
         gsend[pl.ds(chunk * 16, 16)] = turned_cells.astype(BF16).reshape(16, 16, 128)
 
         def send_back(j, carry):
-            q = chunk * 16 + (orb % 16 + j) % 16
-            exchange(gsend.at[q], grecv.at[orb], q, 1).start()
+            other = (place + j) % 16
+            q = other * 4 + chunk
+            exchange(gsend.at[chunk * 16 + other], grecv.at[orb], q, 1).start()
             return carry
 
-        lax.fori_loop(1 if i == 0 else 0, 16, send_back, 0)
-    grecv[orb] = gsend[orb]
+        lax.fori_loop(1 if index == 3 else 0, 16, send_back, 0)
+    grecv[orb] = gsend[groups[3] * 16 + place]
     every = exchange(gsend.at[pl.ds(0, 63)], grecv.at[pl.ds(0, 63)], orb, 1)
     every.wait()
     for g in range(4):
@@ -528,8 +568,11 @@
     consts = [jnp.asarray(t) for t in tables()]
     smem = pl.BlockSpec(memory_space=pltpu.SMEM)
     vmem = pl.BlockSpec(memory_space=pltpu.VMEM)
+    anywhere = pl.BlockSpec(memory_space=pl.ANY)
     dma = pltpu.SemaphoreType.DMA
-    scratch = [
+    placed = [((K, ROWS, CZ), F32), ((ROWS, CZ), F32), ((128, 512), F32)]
+    placed += [(t.shape, BF16) for t in consts]
+    scratch = [pltpu.VMEM(shape, kind) for shape, kind in placed] + [
         pltpu.VMEM((512, 128), F32),
         pltpu.VMEM((8, NP, 16, 128), F32),
         pltpu.VMEM((NP, ROWS, 128), F32),
@@ -568,11 +611,12 @@
         dma((2,)),
         dma((2,)),
         dma((2,)),
+        dma((12,)),
     ]
     result = pl.pallas_call(
         kernel,
         out_shape=jax.ShapeDtypeStruct((K, ROWS, CZ), BF16),
-        in_specs=[smem] * 4 + [vmem] * (4 + len(consts)),
+        in_specs=[smem] * 4 + [anywhere] * 3 + [vmem] + [anywhere] * len(consts),
         out_specs=vmem,
         scratch_shapes=scratch,
         compiler_params=pltpu.CompilerParams(

time: 83.7 us -> 81 us (0.968)
  Pallas kernels: 81.8 us -> 79.1 us
    pallas_call x1, Pallas kernels: 81.8 us -> 79.1 us  [body(): pl.pallas_call(kernel, out_shape=jax.ShapeDtypeStruct((K, ROWS, CZ), BF16...]
where the time goes in v2:
time: 81 us; the launch traced here: 80.8 us
  Pallas kernels  79.1 us (98%)
  local copies, waits for them, and re-layouts  1.65 us (2%)
    pallas_call x1, Pallas kernels, body(): pl.pallas_call(kernel, out_shape=jax.ShapeDtypeStruct((K, ROWS, CZ), BF16...  79.1 us
    unnamed x1, local copies, waits for them, and re-layouts  1.65 us

profile of v2, /device:TPU:33, one launch (start us, length us, event | category | flops | bytes accessed | tf_op | source)
XLA Modules:
  0.0 80.8 jit_solution(3813702592465231999)
XLA Ops:
  0.0 79.1 %filter_rotate.1 = bf16[5,192,128]{2,1,0:T(8,128)(2,1)} custom-call(s32[16]{0:T(128)} %first_s.1, s32[16]{0:T(128)} %second_s.1, s32[16]{0:T(128)} %third_s.1, f32[8]{0:T(128)} %energy_s.1, f32[5,192,128]{2,1,0:T(8,128)} %bitcast.5, f32[192,128]{1,0:T(8,128)} %bitcast.7, f32[128,512]{1,0:T(8,128)} %bitcast.6, bf16[5,320]{1,0:T(8,128)(2,1)} %rot_ref.1, ...), custom_call_target="tpu_custom_call" | custom-call | tf_op jit(solution)/shard_map/filter_rotate/pallas_call | solution.py:616
  79.2 1.7 %copy.19 = bf16[1,5,12,16,128]{4,3,2,1,0:T(8,128)(2,1)} copy(bf16[1,5,12,16,128]{4,3,2,1,0:T(8,128)(2,1)} %bitcast.4) | data formatting | bytes 491520

commit v3 on v2

--- a/solution.py
+++ b/solution.py
@@ -17,7 +17,7 @@
 NP = 8
 NDOM, NORB_DEV = 8, 64
 REACH = 6
-AHEAD = 2
+AHEAD = 1
 WEIGHTS = (
     -5369.0 / 1800.0,
     12.0 / 7.0,
@@ -102,7 +102,13 @@
                 for r in range(3):
                     widen[s, 5 * c + o, s, 3 * o + r] = 1.0
     widen = widen.reshape(256, 256).astype(jnp.bfloat16)
-    return own3, both2, line3, ends2, pick_y, pick_z, to_tiles, from_tiles, widen
+    join = np.zeros((K, 128, 128))
+    for k in range(K):
+        for lane in range(128):
+            join[k, lane, 16 * k + lane // 8] = 1.0
+    part = np.ascontiguousarray(join.transpose(2, 0, 1)).reshape(128, K * 128).astype(jnp.bfloat16)
+    join = join.reshape(K * 128, 128).astype(jnp.bfloat16)
+    return own3, both2, line3, ends2, pick_y, pick_z, to_tiles, from_tiles, widen, join, part
 
 
 def split(values):
@@ -115,20 +121,27 @@
     return jnp.dot(a, b, preferred_element_type=F32)
 
 
-def exact_dot(a, b):
-    return jnp.dot(a, b, preferred_element_type=F32, precision=lax.Precision.HIGHEST)
+def thirds(values):
+    high = values.astype(BF16)
+    middle, low = split(values - high.astype(F32))
+    return jnp.concatenate((high, middle, low), axis=0)
+
+
+def exact_dot(values, onehot):
+    parts = dot(thirds(values), onehot)
+    return parts[0:8] + parts[8:16] + parts[16:24]
 
 
 def kernel(
     first_s, second_s, third_s, energy_s,
     x_hbm, v_hbm, proj_hbm, rot_ref,
-    own3_hbm, both2_hbm, line3_hbm, ends2_hbm, pick_y_hbm, pick_z_hbm, to_tiles_hbm, from_tiles_hbm, widen_hbm,
+    own3_hbm, both2_hbm, line3_hbm, ends2_hbm, pick_y_hbm, pick_z_hbm, to_tiles_hbm, from_tiles_hbm, widen_hbm, join_hbm, part_hbm,
     out_ref,
-    x_ref, v_ref, proj_ref, own3, both2, line3, ends2, pick_y, pick_z, to_tiles, from_tiles, widen,
+    x_ref, v_ref, proj_ref, own3, both2, line3, ends2, pick_y, pick_z, to_tiles, from_tiles, widen, join, part,
     turned, across, pxy, szf, y1, acc,
     xsend, ysend, zsend, xrecv, yrecv, zrecv,
     cmsg, crecv, cfull,
-    rtmp, rtile, rring, rother, rall,
+    rtmp, rtile, rother, rall,
     rbig, fb, fsend, frecv, gsend, grecv,
     halo_ssem, halo_rsem, c_ssem, c_rsem, ring_ssem, ring_rsem, hand_ssem, hand_rsem, r_ssem, r_rsem, t_ssem, t_rsem, in_sem,
 ):
@@ -175,10 +188,12 @@
             (
                 (proj_hbm, proj_ref),
                 (x_hbm, x_ref),
+                (join_hbm, join),
                 (pick_y_hbm, pick_y),
                 (pick_z_hbm, pick_z),
                 (own3_hbm, own3),
                 (line3_hbm, line3),
+                (part_hbm, part),
                 (v_hbm, v_ref),
                 (both2_hbm, both2),
                 (ends2_hbm, ends2),
@@ -256,15 +271,14 @@
     szf[0] = onehot.astype(BF16)
     szf[1] = onehot.T.astype(BF16)
 
-    lane_128 = lax.broadcasted_iota(jnp.int32, (128, 128), 1)
-
     def partial_coefficients(source, k):
         high, low = split(source[k])
         picked = dot(high, szf[0]) + dot(low, szf[0])
         sums = [jnp.sum(picked * pxy[p], axis=0, keepdims=True) for p in range(NP)]
-        own = jnp.concatenate(sums, axis=0)
-        gather = jnp.where(zrow // 8 + 16 * k == lane_128, 1.0, 0.0)
-        return exact_dot(own, gather)
+        return jnp.concatenate(sums, axis=0)
+
+    def pack_coefficients(parts):
+        return exact_dot(jnp.concatenate(parts, axis=1), join[...])
 
     def hold_coefficients(packed, slot):
         cmsg[slot] = packed
@@ -299,9 +313,9 @@
         for i in range(1, NDOM):
             total = total + crecv[slot, i]
         total = total * energy
+        spread = exact_dot(total, part[...])
         for k in range(K):
-            gather = jnp.where(zrow == lane_128 // 8 + 16 * k, 1.0, 0.0)
-            cfull[k] = exact_dot(total, gather)
+            cfull[k] = spread[:, 128 * k : 128 * k + 128]
 
     def pack_halo(values, level, k):
         high = values.astype(BF16)
@@ -352,12 +366,16 @@
         return total + flat
 
     inputs[1].wait()
-    packed = jnp.zeros((8, 128), F32)
-    for k in range(K):
-        packed = packed + partial_coefficients(x_ref, k)
-    hold_coefficients(packed, 0)
     inputs[2].wait()
+    parts = []
+    high, low = split(x_ref[...].reshape(K * ROWS, CZ))
+    picked = (dot(high, szf[0]) + dot(low, szf[0])).reshape(K, ROWS, CZ)
+    for k in range(K):
+        sums = [jnp.sum(picked[k] * pxy[p], axis=0, keepdims=True) for p in range(NP)]
+        parts.append(jnp.concatenate(sums, axis=0))
+    hold_coefficients(pack_coefficients(parts), 0)
     inputs[3].wait()
+    inputs[4].wait()
     for k in range(K):
         pack_halo(x_ref[k], 0, k)
     rtmp[...] = jnp.zeros((16, 128), F32)
@@ -370,7 +388,32 @@
 
     pl.semaphore_wait(barrier, 31 + 7 + 2)
     send_coefficients(0)
-    for k in range(K):
+
+    ring_copy = pltpu.make_async_remote_copy(
+        src_ref=rtile,
+        dst_ref=rother,
+        send_sem=ring_ssem,
+        recv_sem=ring_rsem,
+        device_id=ring_peer(-1),
+        device_id_type=MESH,
+    )
+    hands = [
+        pltpu.make_async_remote_copy(
+            src_ref=rother,
+            dst_ref=rother,
+            send_sem=hand_ssem.at[i],
+            recv_sem=hand_rsem,
+            device_id=dom_peer(i + 1),
+            device_id_type=MESH,
+        )
+        for i in range(NDOM - 1)
+    ]
+
+    @pl.when(dom == 0)
+    def _():
+        ring_copy.start()
+
+    for k in range(2):
         for copy in halo_copies(0, k):
             copy.start()
 
@@ -390,38 +433,47 @@
 
     lax.fori_loop(1, 32, send_rows, 0)
 
-    for copy in inputs[4:]:
+    @pl.when(dom == NDOM - 1)
+    def _():
+        ring_copy.wait_recv()
+        for copy in hands:
+            copy.start()
+
+    for copy in inputs[5:]:
         copy.wait()
     for k in range(K):
         own_part(x_ref, k)
+        if k + 2 < K:
+            for copy in halo_copies(0, k):
+                copy.wait_send()
+            for copy in halo_copies(0, k + 2):
+                copy.start()
 
     await_coefficients(0)
-    ring_copies = []
-    for index, step in enumerate((1, -1)):
-        ring_copies.append(
-            pltpu.make_async_remote_copy(
-                src_ref=rtile,
-                dst_ref=rring.at[index],
-                send_sem=ring_ssem.at[index],
-                recv_sem=ring_rsem.at[index],
-                device_id=ring_peer(step),
-                device_id_type=MESH,
-            )
-        )
-        ring_copies[-1].start()
-
-    hands = [
-        pltpu.make_async_remote_copy(
-            src_ref=rring.at[1],
-            dst_ref=rother,
-            send_sem=hand_ssem.at[i],
-            recv_sem=hand_rsem,
-            device_id=dom_peer(i + 1),
-            device_id_type=MESH,
-        )
-        for i in range(NDOM - 1)
-    ]
-    packed = jnp.zeros((8, 128), F32)
+
+    @pl.when(dom == 0)
+    def _():
+        ring_copy.wait_send()
+
+    @pl.when(dom == NDOM - 1)
+    def _():
+        for copy in hands:
+            copy.wait_send()
+
+    @pl.when(dom != NDOM - 1)
+    def _():
+        hands[0].wait_recv()
+
+    orb_other = orb + 2 - 4 * zhi
+    rall[orb_other] = rother[...]
+
+    def send_other(i, carry):
+        tile_copy(rother, i, orb_other, 1).start()
+        return carry
+
+    lax.fori_loop(1, 32, send_other, 0)
+
+    parts = []
     for k in range(K):
         nonlocal_part(k)
         y1[k] = halo_part(0, k) * (1.0 / WIDTH)
@@ -429,18 +481,9 @@
         if k < AHEAD:
             for copy in halo_copies(1, k):
                 copy.start()
-        packed = packed + partial_coefficients(y1, k)
-        if k == AHEAD - 1:
-            for copy in ring_copies:
-                copy.wait()
-
-            @pl.when(dom == NDOM - 1)
-            def _():
-                for copy in hands:
-                    copy.start()
-                rother[...] = rring[1]
-
-    hold_coefficients(packed, 1)
+        parts.append(partial_coefficients(y1, k))
+
+    hold_coefficients(pack_coefficients(parts), 1)
     send_coefficients(1)
     for k in range(AHEAD, K):
         for copy in halo_copies(1, k):
@@ -449,30 +492,12 @@
     for k in range(K):
         own_part(y1, k)
 
-    @pl.when(dom == NDOM - 1)
-    def _():
-        for copy in hands:
-            copy.wait_send()
-
-    @pl.when(dom != NDOM - 1)
-    def _():
-        hands[0].wait_recv()
-
-    orb_other = orb + 2 - 4 * zhi
-    rall[orb_other] = rother[...]
-
-
-    def send_other(i, carry):
-        tile_copy(rother, i, orb_other, 1).start()
-        return carry
-
-    lax.fori_loop(1, 32, send_other, 0)
     await_coefficients(1)
 
     for k in range(K):
         nonlocal_part(k)
     for level in range(2):
-        for k in range(K):
+        for k in range(K - 2 if level == 0 else 0, K):
             for copy in halo_copies(level, k):
                 copy.wait_send()
     for k in range(K):
@@ -481,6 +506,10 @@
         rows = [fb[o, pl.ds((4 * r + g) * 16, 16), :] for o in range(K) for r in range(3)]
         tiles = dot(to_tiles[...], jnp.concatenate(rows, axis=0))
         fsend[16 * g : 16 * g + 16] = tiles.astype(BF16).reshape(16, 16, 128)
+
+    for wave in range(2):
+        every = tile_copy(rall.at[pl.ds(0, 31)], 1, pl.ds(0, 31), wave)
+        every.wait()
 
     def exchange(source, target, q, wave):
         return pltpu.make_async_remote_copy(
@@ -506,9 +535,6 @@
         lax.fori_loop(1 if index == 3 else 0, 16, send_cells, 0)
     frecv[orb] = fsend[orb]
 
-    for wave in range(2):
-        every = tile_copy(rall.at[pl.ds(0, 31)], 1, pl.ds(0, 31), wave)
-        every.wait()
     rows_all = rall[...].reshape(1024, 128)
     row_e = lax.broadcasted_iota(jnp.int32, (256, 128), 0)
     lane_e = lax.broadcasted_iota(jnp.int32, (256, 128), 1)
@@ -590,7 +616,6 @@
         pltpu.VMEM((K, 8, 128), F32),
         pltpu.VMEM((16, 128), F32),
         pltpu.VMEM((16, 128), BF16),
-        pltpu.VMEM((2, 16, 128), BF16),
         pltpu.VMEM((16, 128), BF16),
         pltpu.VMEM((NORB_DEV, 16, 128), BF16),
         pltpu.VMEM((1024, 1024), BF16),
@@ -603,15 +628,15 @@
         dma((2, 3, K)),
         dma((2,)),
         dma((2,)),
-        dma((2,)),
-        dma((2,)),
+        dma(()),
+        dma(()),
         dma((NDOM - 1,)),
         dma(()),
         dma((2,)),
         dma((2,)),
         dma((2,)),
         dma((2,)),
-        dma((12,)),
+        dma((14,)),
     ]
     result = pl.pallas_call(
         kernel,

time: 81 us -> 80.1 us (0.989)
  Pallas kernels: 79.1 us -> 78.2 us
    pallas_call x1, Pallas kernels: 79.1 us -> 78.2 us  [body(): pl.pallas_call(kernel, out_shape=jax.ShapeDtypeStruct((K, ROWS, CZ), BF16...]
where the time goes in v3:
time: 80.1 us; the launch traced here: 79.9 us
  Pallas kernels  78.2 us (98%)
  local copies, waits for them, and re-layouts  1.65 us (2%)
    pallas_call x1, Pallas kernels, body(): pl.pallas_call(kernel, out_shape=jax.ShapeDtypeStruct((K, ROWS, CZ), BF16...  78.2 us
    unnamed x1, local copies, waits for them, and re-layouts  1.65 us

profile of v3, /device:TPU:33, one launch (start us, length us, event | category | flops | bytes accessed | tf_op | source)
XLA Modules:
  0.0 79.9 jit_solution(244032846954792101)
XLA Ops:
  0.0 78.2 %filter_rotate.1 = bf16[5,192,128]{2,1,0:T(8,128)(2,1)} custom-call(s32[16]{0:T(128)} %first_s.1, s32[16]{0:T(128)} %second_s.1, s32[16]{0:T(128)} %third_s.1, f32[8]{0:T(128)} %energy_s.1, f32[5,192,128]{2,1,0:T(8,128)} %bitcast.5, f32[192,128]{1,0:T(8,128)} %bitcast.7, f32[128,512]{1,0:T(8,128)} %bitcast.6, bf16[5,320]{1,0:T(8,128)(2,1)} %rot_ref.1, ...), custom_call_target="tpu_custom_call" | custom-call | tf_op jit(solution)/shard_map/filter_rotate/pallas_call | solution.py:641
  78.2 1.7 %copy.21 = bf16[1,5,12,16,128]{4,3,2,1,0:T(8,128)(2,1)} copy(bf16[1,5,12,16,128]{4,3,2,1,0:T(8,128)(2,1)} %bitcast.4) | data formatting | bytes 491520

commit v4 on v3

--- a/solution.py
+++ b/solution.py
@@ -451,28 +451,6 @@
 
     await_coefficients(0)
 
-    @pl.when(dom == 0)
-    def _():
-        ring_copy.wait_send()
-
-    @pl.when(dom == NDOM - 1)
-    def _():
-        for copy in hands:
-            copy.wait_send()
-
-    @pl.when(dom != NDOM - 1)
-    def _():
-        hands[0].wait_recv()
-
-    orb_other = orb + 2 - 4 * zhi
-    rall[orb_other] = rother[...]
-
-    def send_other(i, carry):
-        tile_copy(rother, i, orb_other, 1).start()
-        return carry
-
-    lax.fori_loop(1, 32, send_other, 0)
-
     parts = []
     for k in range(K):
         nonlocal_part(k)
@@ -488,6 +466,28 @@
     for k in range(AHEAD, K):
         for copy in halo_copies(1, k):
             copy.start()
+
+    @pl.when(dom == 0)
+    def _():
+        ring_copy.wait_send()
+
+    @pl.when(dom == NDOM - 1)
+    def _():
+        for copy in hands:
+            copy.wait_send()
+
+    @pl.when(dom != NDOM - 1)
+    def _():
+        hands[0].wait_recv()
+
+    orb_other = orb + 2 - 4 * zhi
+    rall[orb_other] = rother[...]
+
+    def send_other(i, carry):
+        tile_copy(rother, i, orb_other, 1).start()
+        return carry
+
+    lax.fori_loop(1, 32, send_other, 0)
 
     for k in range(K):
         own_part(y1, k)

time: 80.1 us -> 79.6 us (level)
  no operation moved by 1% of the time
where the time goes in v4:
time: 79.6 us; the launch traced here: 79.4 us
  Pallas kernels  77.8 us (98%)
  local copies, waits for them, and re-layouts  1.65 us (2%)
    pallas_call x1, Pallas kernels, body(): pl.pallas_call(kernel, out_shape=jax.ShapeDtypeStruct((K, ROWS, CZ), BF16...  77.8 us
    unnamed x1, local copies, waits for them, and re-layouts  1.65 us

profile of v4, /device:TPU:33, one launch (start us, length us, event | category | flops | bytes accessed | tf_op | source)
XLA Modules:
  0.0 79.4 jit_solution(16261786244425046276)
XLA Ops:
  0.0 77.8 %filter_rotate.1 = bf16[5,192,128]{2,1,0:T(8,128)(2,1)} custom-call(s32[16]{0:T(128)} %first_s.1, s32[16]{0:T(128)} %second_s.1, s32[16]{0:T(128)} %third_s.1, f32[8]{0:T(128)} %energy_s.1, f32[5,192,128]{2,1,0:T(8,128)} %bitcast.5, f32[192,128]{1,0:T(8,128)} %bitcast.7, f32[128,512]{1,0:T(8,128)} %bitcast.6, bf16[5,320]{1,0:T(8,128)(2,1)} %rot_ref.1, ...), custom_call_target="tpu_custom_call" | custom-call | tf_op jit(solution)/shard_map/filter_rotate/pallas_call | solution.py:641
  77.8 1.7 %copy.21 = bf16[1,5,12,16,128]{4,3,2,1,0:T(8,128)(2,1)} copy(bf16[1,5,12,16,128]{4,3,2,1,0:T(8,128)(2,1)} %bitcast.4) | data formatting | bytes 491520

commit v5 on v4

--- a/solution.py
+++ b/solution.py
@@ -496,10 +496,6 @@
 
     for k in range(K):
         nonlocal_part(k)
-    for level in range(2):
-        for k in range(K - 2 if level == 0 else 0, K):
-            for copy in halo_copies(level, k):
-                copy.wait_send()
     for k in range(K):
         fb[k] = (halo_part(1, k) * (2.0 / WIDTH) - x_ref[k]).astype(BF16)
     for g in range(4):
@@ -534,6 +530,11 @@
 
         lax.fori_loop(1 if index == 3 else 0, 16, send_cells, 0)
     frecv[orb] = fsend[orb]
+
+    for level in range(2):
+        for k in range(K - 2 if level == 0 else 0, K):
+            for copy in halo_copies(level, k):
+                copy.wait_send()
 
     rows_all = rall[...].reshape(1024, 128)
     row_e = lax.broadcasted_iota(jnp.int32, (256, 128), 0)

time: 79.6 us -> 80.6 us (1.013)
  Pallas kernels: 77.8 us -> 78.8 us
    pallas_call x1, Pallas kernels: 77.8 us -> 78.8 us  [body(): pl.pallas_call(kernel, out_shape=jax.ShapeDtypeStruct((K, ROWS, CZ), BF16...]
where the time goes in v5:
time: 80.6 us; the launch traced here: 80.4 us
  Pallas kernels  78.8 us (98%)
  local copies, waits for them, and re-layouts  1.65 us (2%)
    pallas_call x1, Pallas kernels, body(): pl.pallas_call(kernel, out_shape=jax.ShapeDtypeStruct((K, ROWS, CZ), BF16...  78.8 us
    unnamed x1, local copies, waits for them, and re-layouts  1.65 us

profile of v5, /device:TPU:33, one launch (start us, length us, event | category | flops | bytes accessed | tf_op | source)
XLA Modules:
  0.0 80.4 jit_solution(7921117451155684728)
XLA Ops:
  0.0 78.8 %filter_rotate.1 = bf16[5,192,128]{2,1,0:T(8,128)(2,1)} custom-call(s32[16]{0:T(128)} %first_s.1, s32[16]{0:T(128)} %second_s.1, s32[16]{0:T(128)} %third_s.1, f32[8]{0:T(128)} %energy_s.1, f32[5,192,128]{2,1,0:T(8,128)} %bitcast.5, f32[192,128]{1,0:T(8,128)} %bitcast.7, f32[128,512]{1,0:T(8,128)} %bitcast.6, bf16[5,320]{1,0:T(8,128)(2,1)} %rot_ref.1, ...), custom_call_target="tpu_custom_call" | custom-call | tf_op jit(solution)/shard_map/filter_rotate/pallas_call | solution.py:642
  78.8 1.7 %copy.21 = bf16[1,5,12,16,128]{4,3,2,1,0:T(8,128)(2,1)} copy(bf16[1,5,12,16,128]{4,3,2,1,0:T(8,128)(2,1)} %bitcast.4) | data formatting | bytes 491520

commit v6 on v4

--- a/solution.py
+++ b/solution.py
@@ -467,6 +467,9 @@
         for copy in halo_copies(1, k):
             copy.start()
 
+    for k in range(K):
+        own_part(y1, k)
+
     @pl.when(dom == 0)
     def _():
         ring_copy.wait_send()
@@ -488,9 +491,6 @@
         return carry
 
     lax.fori_loop(1, 32, send_other, 0)
-
-    for k in range(K):
-        own_part(y1, k)
 
     await_coefficients(1)
 

time: 79.6 us -> 79.6 us (level)
  no operation moved by 1% of the time
where the time goes in v6:
time: 79.6 us; the launch traced here: 79.4 us
  Pallas kernels  77.8 us (98%)
  local copies, waits for them, and re-layouts  1.65 us (2%)
    pallas_call x1, Pallas kernels, body(): pl.pallas_call(kernel, out_shape=jax.ShapeDtypeStruct((K, ROWS, CZ), BF16...  77.8 us
    unnamed x1, local copies, waits for them, and re-layouts  1.65 us

profile of v6, /device:TPU:33, one launch (start us, length us, event | category | flops | bytes accessed | tf_op | source)
XLA Modules:
  0.0 79.4 jit_solution(3878689976560925832)
XLA Ops:
  0.0 77.8 %filter_rotate.1 = bf16[5,192,128]{2,1,0:T(8,128)(2,1)} custom-call(s32[16]{0:T(128)} %first_s.1, s32[16]{0:T(128)} %second_s.1, s32[16]{0:T(128)} %third_s.1, f32[8]{0:T(128)} %energy_s.1, f32[5,192,128]{2,1,0:T(8,128)} %bitcast.5, f32[192,128]{1,0:T(8,128)} %bitcast.7, f32[128,512]{1,0:T(8,128)} %bitcast.6, bf16[5,320]{1,0:T(8,128)(2,1)} %rot_ref.1, ...), custom_call_target="tpu_custom_call" | custom-call | tf_op jit(solution)/shard_map/filter_rotate/pallas_call | solution.py:641
  77.8 1.7 %copy.21 = bf16[1,5,12,16,128]{4,3,2,1,0:T(8,128)(2,1)} copy(bf16[1,5,12,16,128]{4,3,2,1,0:T(8,128)(2,1)} %bitcast.4) | data formatting | bytes 491520
